TPU v7x, 512 devices: a whole 4x4x16 slice. The times are simulated.
512 devices in a mesh: mem: 32 (over x_hi, z), gx: 4 (over x_lo, core), gy: 4 (over y).
Axes of the slice: x: 4 (x_hi: 2, x_lo: 2; x = x_hi * 2 + x_lo), y: 4, z: 16, core: 2. Of those that a mesh axis runs over, the one named last changes fastest.
Arguments:
- control: float32 [64, 1024, 1024], P('mem', 'gx', 'gy'), may hold values from -6 to 6
- ensemble: bfloat16 [64, 1024, 1024], P('mem', 'gx', 'gy'), may hold values from -0.75 to 0.75
- obs_index: int32 [1024, 256], P('gx', 'gy'), may hold values from 0 to 255
- obs_value: float32 [1024, 256], P('gx', 'gy'), may hold values from -12 to 12
- obs_weight: float32 [1024, 256], P('gx', 'gy'), may hold values from 1 to 16
Outputs:
- gradient: float32 [64, 1024, 1024], P('mem', 'gx', 'gy')
Inputs may be any that keep to these rules, and one draw needn't show every extreme that they name: obs_index[r, j] is a column inside the y tile j // 64; several observations may share a cell.
All inputs are finite; a program needn't handle non-finite values.
Results may differ from a plain program's by a relative error of at most 0.0003.
Values sent between devices are 32-bit elements; how exact they have to be, the bound alone decides.
A program may use at most 64 MiB of HBM per device.

v0:
```python
import math
import jax
import jax.numpy as jnp
from jax import lax
from jax.sharding import PartitionSpec as P

LEN = 400
saturation = 1.5
highest = lax.Precision.HIGHEST


def from_behind(value, axis, steps):
    count = lax.axis_size(axis)
    leading, last = (max(0, -steps), min(count, count - steps))
    return lax.ppermute(value, axis, [(source, source + steps) for source in range(leading, last)])


def pair_scale():
    decay_rate = math.exp(-1.0 / LEN)
    return (1.0 - decay_rate * decay_rate) / (1.0 + decay_rate * decay_rate)


def filter_tables(length):
    decay_log = -1.0 / LEN
    unit_gain = math.sqrt(1.0 - math.exp(2.0 * decay_log))
    positions = jnp.arange(length, dtype=jnp.float32)
    offsets = positions[:, None] - positions[None, :]
    forward_matrix = jnp.where(
        offsets >= 0, unit_gain * jnp.exp(jnp.maximum(offsets, 0.0) * decay_log), 0.0
    )
    carry_weights = jnp.exp((positions + 1.0) * decay_log)
    chain_factor = jnp.float32(math.exp(length * decay_log))
    return (forward_matrix, carry_weights, chain_factor)


def sweep_x_forward(grid_field):
    forward_matrix, carry_weights, chain_factor = filter_tables(grid_field.shape[1])
    boundary = jnp.einsum("j,mjc->mc", forward_matrix[-1], grid_field, precision=highest)
    local_part = jnp.einsum("ij,mjc->mic", forward_matrix, grid_field, precision=highest)
    incoming = jnp.zeros_like(boundary)
    for repeat in range(lax.axis_size("gx") - 1):
        incoming = from_behind(chain_factor * incoming + boundary, "gx", 1)
    return local_part + carry_weights[None, :, None] * incoming[:, None, :]


def sweep_x_backward(grid_field):
    forward_matrix, carry_weights, chain_factor = filter_tables(grid_field.shape[1])
    boundary = jnp.einsum("j,mjc->mc", forward_matrix[:, 0], grid_field, precision=highest)
    local_part = jnp.einsum("ji,mjc->mic", forward_matrix, grid_field, precision=highest)
    incoming = jnp.zeros_like(boundary)
    for repeat in range(lax.axis_size("gx") - 1):
        incoming = from_behind(chain_factor * incoming + boundary, "gx", -1)
    return local_part + carry_weights[::-1][None, :, None] * incoming[:, None, :]


def sweep_y_forward(grid_field):
    forward_matrix, carry_weights, chain_factor = filter_tables(grid_field.shape[2])
    boundary = jnp.einsum("mrj,j->mr", grid_field, forward_matrix[-1], precision=highest)
    local_part = jnp.einsum("mrj,ij->mri", grid_field, forward_matrix, precision=highest)
    incoming = jnp.zeros_like(boundary)
    for repeat in range(lax.axis_size("gy") - 1):
        incoming = from_behind(chain_factor * incoming + boundary, "gy", 1)
    return local_part + incoming[:, :, None] * carry_weights[None, None, :]


def sweep_y_backward(grid_field):
    forward_matrix, carry_weights, chain_factor = filter_tables(grid_field.shape[2])
    boundary = jnp.einsum("mrj,j->mr", grid_field, forward_matrix[:, 0], precision=highest)
    local_part = jnp.einsum("mrj,ji->mri", grid_field, forward_matrix, precision=highest)
    incoming = jnp.zeros_like(boundary)
    for repeat in range(lax.axis_size("gy") - 1):
        incoming = from_behind(chain_factor * incoming + boundary, "gy", -1)
    return local_part + incoming[:, :, None] * carry_weights[::-1][None, None, :]


def smooth(grid_field):
    along_x = sweep_x_backward(sweep_x_forward(grid_field))
    return pair_scale() * sweep_y_backward(sweep_y_forward(along_x))


def smooth_adjoint(grid_field):
    along_y = sweep_y_backward(sweep_y_forward(grid_field))
    return pair_scale() * sweep_x_backward(sweep_x_forward(along_y))


def obs_residual(grid_field, columns, values, weights):
    picked = jnp.take_along_axis(grid_field, columns, axis=1)
    misfit = picked - values
    return weights * saturation * jnp.tanh(misfit / saturation)


def place_residual(residual, columns, like_field):
    row_ids = lax.broadcasted_iota(jnp.int32, columns.shape, 0)
    return jnp.zeros_like(like_field).at[row_ids, columns].add(residual)


def on_device(control, ensemble, obs_index, obs_value, obs_weight):
    smoothed = smooth(control)
    partial_value = jnp.sum(ensemble * smoothed, axis=0)
    increment = lax.psum(partial_value, "mem")
    forcing = place_residual(
        obs_residual(increment, obs_index, obs_value, obs_weight), obs_index, increment
    )
    adjoint = smooth_adjoint(ensemble * forcing[None])
    return control + adjoint


def solution(mesh):
    return jax.shard_map(
        on_device,
        mesh=mesh,
        in_specs=(
            P("mem", "gx", "gy"),
            P("mem", "gx", "gy"),
            P("gx", "gy"),
            P("gx", "gy"),
            P("gx", "gy"),
        ),
        out_specs=P("mem", "gx", "gy"),
        check_vma=False,
    )
```

profile of v0, /device:TPU:1, one launch (start us, length us, event | category | flops | bytes accessed | tf_op | source)
XLA Modules:
  0.0 676.7 jit_solution(3496676984004328318)
XLA Ops:
  8.2 4.5 collective-permute-start
  12.7 4.3 collective-permute-done
  20.1 3.8 collective-permute-start.2
  26.9 3.5 collective-permute-done.3
  32.4 3.0 collective-permute-done.4
  37.4 2.9 collective-permute-done.5
  44.4 3.6 collective-permute-start.7
  48.7 3.7 collective-permute-start.8
  55.4 3.0 collective-permute-done.9
  59.7 3.0 collective-permute-done.10
  64.2 2.9 collective-permute-done.11
  69.3 289.4 %all-reduce.2.cloned.1.call-done = f32[256,256]{1,0:T(8,128)} async-done(((f32[256,256]{1,0:T(8,128)}), f32[256,256]{1,0:T(8,128)}) %all-reduce.2.cloned.1.call-update) | async-done | bytes 262160 | tf_op jit(solution)/shard_map/psum | solution.py:100
  358.8 109.0 %gather_fusion = f32[16384]{0:T(1024)S(1)} fusion(f32[256,256]{1,0:T(8,128)} %all-reduce.2.cloned.1.call-done, s32[16384]{0:T(1024)S(1)} %reshape.46), kind=kCustom, calls=%fused_computation | custom fusion | bytes 262144 | tf_op jit(solution)/shard_map/jit(take_along_axis)/gather | solution.py:87
  468.2 113.5 %scatter_custom_fusion = f32[65536]{0:T(1024)S(1)} fusion(s32[16384]{0:T(1024)S(1)} %reshape.52, f32[16384]{0:T(1024)S(1)} %reshape.54, f32[]{:T(128)} %constant.12.clone.1), kind=kCustom, calls=%fused_computation.52 | custom fusion | flops 16384 | bytes 262148
  582.4 3.1 collective-permute-start.12
  586.2 3.6 collective-permute-start.13
  590.5 3.6 collective-permute-start.14
  597.1 3.0 collective-permute-done.15
  601.5 3.0 collective-permute-done.16
  610.1 30.8 %collective-permute-start.18 = (f32[2,256]{1,0:T(2,128)S(1)}, f32[2,256]{1,0:T(2,128)S(1)}, u32[]{:S(2)}, u32[]{:S(2)}) collective-permute-start(f32[2,256]{1,0:T(2,128)S(1)} %bitcast.136), channel_id=1, source_target_pairs={{0,4},{4,8},{8,12},{1,5},{5,9},{9,13},{2,6},{6,10},{10,14},{3,7},{... | collective-permute-start | bytes 6152 | tf_op jit(solution)/shard_map/ppermute | solution.py:15
  641.7 4.2 collective-permute-start.19
  646.6 4.2 collective-permute-start.20
  654.5 3.5 collective-permute-done.21
  660.0 3.0 collective-permute-done.22
  (106 shorter events, 50.8 us)
Async XLA Ops:
  6.5 352.2 %all-reduce.2.cloned.1.call-start = ((), (), s32[]{:S(2)}) async-start(), calls=%async_computation | async-start | bytes 524288 | tf_op jit(solution)/shard_map/psum | solution.py:100
  8.2 8.8 %collective-permute-start = (f32[2,256]{1,0:T(2,128)S(1)}, f32[2,256]{1,0:T(2,128)S(1)}, u32[]{:S(2)}, u32[]{:S(2)}) collective-permute-start(f32[2,256]{1,0:T(2,128)S(1)} %bitcast.130), channel_id=1, source_target_pairs={{0,4},{4,8},{8,12},{1,5},{5,9},{9,13},{2,6},{6,10},{10,14},{3,7},{... | collective-permute-start | bytes 6152 | tf_op jit(solution)/shard_map/ppermute | solution.py:15
  17.0 3.0 collective-permute-start.1
  20.1 4.5 collective-permute-start.2
  25.0 5.4 collective-permute-start.3
  30.5 4.9 collective-permute-start.4
  35.4 4.9 collective-permute-start.5
  44.4 4.3 collective-permute-start.7
  48.7 4.7 collective-permute-start.8
  54.1 4.3 collective-permute-start.9
  58.4 4.3 collective-permute-start.10
  62.7 4.3 collective-permute-start.11
  582.4 3.8 collective-permute-start.12
  586.2 4.3 collective-permute-start.13
  590.5 4.6 collective-permute-start.14
  595.8 4.3 collective-permute-start.15
  600.2 4.3 collective-permute-start.16
  604.5 4.3 collective-permute-start.17
  610.1 31.6 %collective-permute-start.18 = (f32[2,256]{1,0:T(2,128)S(1)}, f32[2,256]{1,0:T(2,128)S(1)}, u32[]{:S(2)}, u32[]{:S(2)}) collective-permute-start(f32[2,256]{1,0:T(2,128)S(1)} %bitcast.136), channel_id=1, source_target_pairs={{0,4},{4,8},{8,12},{1,5},{5,9},{9,13},{2,6},{6,10},{10,14},{3,7},{... | collective-permute-start | bytes 6152 | tf_op jit(solution)/shard_map/ppermute | solution.py:15
  641.7 4.9 collective-permute-start.19
  646.6 4.9 collective-permute-start.20
  652.6 5.4 collective-permute-start.21
  658.1 4.9 collective-permute-start.22
  663.0 4.9 collective-permute-start.23
  (7 other events, 830.2 us)
Sparse Core Ops, SparseCore 0:
  68.9 289.8 all-reduce.1
where the time goes:
time: 677 us
  waiting for transfers between devices  336 us (50%)
  other arithmetic  114 us (17%)
  local copies, waits for them, and re-layouts  112 us (17%)
  starting transfers between devices  88.2 us (13%)
  between operations  13.9 us (2%)
  matrix products  12.1 us (2%)
    psum x1, waiting for transfers between devices, on_device(): increment = lax.psum(partial_value, 'mem')  289 us
    unnamed x4, other arithmetic  114 us
    gather x3, local copies, waits for them, and re-layouts, obs_residual(): picked = jnp.take_along_axis(grid_field, columns, axis=1)  109 us
    ppermute x24, starting transfers between devices, from_behind(): lax.ppermute(value, axis, [(source, source + steps) for source in range(l...  88.2 us
    ppermute x24, waiting for transfers between devices, from_behind(): lax.ppermute(value, axis, [(source, source + steps) for source in range(l...  46.8 us
  transfers between devices with their start and end apart: 25, of which 23 were waited for; matrix products, arithmetic and copies ran while one was open for 1% of the time, Pallas kernels for 0%

commit v1 on v0

--- a/solution.py
+++ b/solution.py
@@ -97,7 +97,7 @@
 def on_device(control, ensemble, obs_index, obs_value, obs_weight):
     smoothed = smooth(control)
     partial_value = jnp.sum(ensemble * smoothed, axis=0)
-    increment = lax.psum(partial_value, "mem")
+    increment = jnp.sum(lax.all_gather(partial_value, "mem"), axis=0)
     forcing = place_residual(
         obs_residual(increment, obs_index, obs_value, obs_weight), obs_index, increment
     )

time: 677 us -> 616 us (0.910)
  waiting for transfers between devices: 336 us -> 253 us
  local copies, waits for them, and re-layouts: 112 us -> 141 us
  starting transfers between devices: 88.2 us -> 76.7 us
    psum x1 -> x0, waiting for transfers between devices: 289 us -> none  [on_device(): increment = lax.psum(partial_value, 'mem')]
    all_gather x0 -> x1, waiting for transfers between devices: none -> 207 us  [on_device(): increment = jnp.sum(lax.all_gather(partial_value, 'mem'), axis=0)]
    gather x3, local copies, waits for them, and re-layouts: 109 us -> 131 us  [obs_residual(): picked = jnp.take_along_axis(grid_field, columns, axis=1)]
    ppermute x24, starting transfers between devices: 88.2 us -> 76.7 us  [from_behind(): lax.ppermute(value, axis, [(source, source + steps) for source in range(l...]
    unnamed x16 -> x15, local copies, waits for them, and re-layouts: 0.54 us -> 8.31 us
  transfers between devices with their start and end apart: 25 -> 25, of which waited for: 23 -> 22; matrix products, arithmetic and copies ran while one was open for 1% -> 1% of each run, Pallas kernels for 0% -> 0%
where the time goes in v1:
time: 616 us; the launch traced here: 615 us
  waiting for transfers between devices  253 us (41%)
  local copies, waits for them, and re-layouts  141 us (23%)
  other arithmetic  117 us (19%)
  starting transfers between devices  76.7 us (12%)
  between operations  13.9 us (2%)
  matrix products  13.8 us (2%)
    all_gather x1, waiting for transfers between devices, on_device(): increment = jnp.sum(lax.all_gather(partial_value, 'mem'), axis=0)  207 us
    gather x3, local copies, waits for them, and re-layouts, obs_residual(): picked = jnp.take_along_axis(grid_field, columns, axis=1)  131 us
    unnamed x4, other arithmetic  114 us
    ppermute x24, starting transfers between devices, from_behind(): lax.ppermute(value, axis, [(source, source + steps) for source in range(l...  76.7 us
    ppermute x24, waiting for transfers between devices, from_behind(): lax.ppermute(value, axis, [(source, source + steps) for source in range(l...  45.3 us
  transfers between devices with their start and end apart: 25, of which 22 were waited for; matrix products, arithmetic and copies ran while one was open for 1% of the time, Pallas kernels for 0%

profile of v1, /device:TPU:1, one launch (start us, length us, event | category | flops | bytes accessed | tf_op | source)
XLA Modules:
  0.0 614.8 jit_solution(8912696445347619953)
XLA Ops:
  8.2 4.5 collective-permute-start
  12.7 4.3 collective-permute-done
  20.7 3.1 collective-permute-start.2
  26.9 3.5 collective-permute-done.3
  32.4 3.0 collective-permute-done.4
  44.4 3.6 collective-permute-start.7
  48.7 3.7 collective-permute-start.8
  55.3 3.0 collective-permute-done.9
  59.7 3.0 collective-permute-done.10
  70.0 207.5 %all-gather.3.cloned.1.call-done = f32[8192,256]{0,1:T(8,128)} async-done(((f32[256,256]{0,1:T(8,128)}), f32[8192,256]{0,1:T(8,128)}) %all-gather.3.cloned.1.call-update) | async-done | bytes 8388624 | tf_op jit(solution)/shard_map/all_gather | solution.py:100
  277.5 6.8 %copy.213 = f32[32,8,32,256]{3,2,1,0:T(8,128)S(1)} copy(f32[32,8,32,256]{3,1,2,0:T(8,128)} %bitcast.131) | data formatting | bytes 16777216
  286.3 130.6 %gather_fusion = f32[16384]{0:T(1024)S(1)} fusion(f32[256,256]{0,1:T(8,128)S(1)} %bitcast_reduce_fusion, s32[16384]{0:T(1024)S(1)} %reshape.46), kind=kCustom, calls=%fused_computation | custom fusion | bytes 262144 | tf_op jit(solution)/shard_map/jit(take_along_axis)/gather | solution.py:87
  417.3 113.5 %scatter_custom_fusion = f32[65536]{0:T(1024)S(1)} fusion(s32[16384]{0:T(1024)S(1)} %reshape.52, f32[16384]{0:T(1024)S(1)} %reshape.54, f32[]{:T(128)} %constant.12.clone.1), kind=kCustom, calls=%fused_computation.53 | custom fusion | flops 16384 | bytes 262148
  531.5 3.1 collective-permute-start.12
  535.3 3.6 collective-permute-start.13
  539.6 3.6 collective-permute-start.14
  546.2 3.0 collective-permute-done.15
  550.6 3.0 collective-permute-done.16
  554.9 3.0 collective-permute-done.17
  559.2 19.8 %collective-permute-start.18 = (f32[2,256]{1,0:T(2,128)S(1)}, f32[2,256]{1,0:T(2,128)S(1)}, u32[]{:S(2)}, u32[]{:S(2)}) collective-permute-start(f32[2,256]{1,0:T(2,128)S(1)} %bitcast.142), channel_id=1, source_target_pairs={{0,4},{4,8},{8,12},{1,5},{5,9},{9,13},{2,6},{6,10},{10,14},{3,7},{... | collective-permute-start | bytes 6152 | tf_op jit(solution)/shard_map/ppermute | solution.py:15
  579.8 4.2 collective-permute-start.19
  584.7 4.4 collective-permute-start.20
  592.6 3.5 collective-permute-done.21
  598.0 3.0 collective-permute-done.22
  (105 shorter events, 56.6 us)
Async XLA Ops:
  6.5 271.0 %all-gather.3.cloned.1.call-start = ((), (), s32[]{:S(2)}) async-start(), calls=%async_computation | async-start | bytes 8650752 | tf_op jit(solution)/shard_map/all_gather | solution.py:100
  8.2 8.8 %collective-permute-start = (f32[2,256]{1,0:T(2,128)S(1)}, f32[2,256]{1,0:T(2,128)S(1)}, u32[]{:S(2)}, u32[]{:S(2)}) collective-permute-start(f32[2,256]{1,0:T(2,128)S(1)} %bitcast.136), channel_id=1, source_target_pairs={{0,4},{4,8},{8,12},{1,5},{5,9},{9,13},{2,6},{6,10},{10,14},{3,7},{... | collective-permute-start | bytes 6152 | tf_op jit(solution)/shard_map/ppermute | solution.py:15
  17.0 3.7 collective-permute-start.1
  20.7 3.8 collective-permute-start.2
  25.0 5.4 collective-permute-start.3
  30.5 4.9 collective-permute-start.4
  35.4 4.9 collective-permute-start.5
  44.4 4.3 collective-permute-start.7
  48.7 4.7 collective-permute-start.8
  54.0 4.3 collective-permute-start.9
  58.4 4.3 collective-permute-start.10
  62.7 4.3 collective-permute-start.11
  531.5 3.8 collective-permute-start.12
  535.3 4.3 collective-permute-start.13
  539.6 4.6 collective-permute-start.14
  544.9 4.3 collective-permute-start.15
  549.3 4.3 collective-permute-start.16
  553.6 4.3 collective-permute-start.17
  559.2 20.5 %collective-permute-start.18 = (f32[2,256]{1,0:T(2,128)S(1)}, f32[2,256]{1,0:T(2,128)S(1)}, u32[]{:S(2)}, u32[]{:S(2)}) collective-permute-start(f32[2,256]{1,0:T(2,128)S(1)} %bitcast.142), channel_id=1, source_target_pairs={{0,4},{4,8},{8,12},{1,5},{5,9},{9,13},{2,6},{6,10},{10,14},{3,7},{... | collective-permute-start | bytes 6152 | tf_op jit(solution)/shard_map/ppermute | solution.py:15
  579.8 4.9 collective-permute-start.19
  584.7 4.9 collective-permute-start.20
  590.7 5.4 collective-permute-start.21
  596.1 4.9 collective-permute-start.22
  601.0 4.9 collective-permute-start.23
  (6 other events, 707.1 us)
Sparse Core Ops, SparseCore 0:
  68.7 208.7 all-gather.2
